TPU v7x, 256 devices: a whole 4x4x8 slice. The times are simulated.
256 devices in a mesh: row: 8 (over y, core), col: 8 (over x, z_hi), rep: 4 (over z_lo).
Axes of the slice: x: 4, y: 4, z: 8 (z_hi: 2, z_lo: 4; z = z_hi * 4 + z_lo), core: 2. Of those that a mesh axis runs over, the one named last changes fastest.
Arguments:
- features: float32 [256, 32768], P('rep', ('col', 'row')), may hold values from -6 to 6
- weight: float32 [256, 256], replicated, may hold values from -0.375 to 0.375
- cotangent: float32 [256, 32768], P('rep', ('row', 'col')), may hold values from -6 to 6
- tile_values: float32 [10240, 128, 128], P(('row', 'col')), may hold values from -0.078125 to 0.078125
- tile_row: int32 [10240], P(('row', 'col')), may hold values from 0 to 31
- tile_col: int32 [10240], P(('row', 'col')), may hold values from 0 to 31
- tile_kind: int32 [10240], P(('row', 'col')), may hold values from 0 to 159
- tile_count: int32 [64], P(('row', 'col')), may hold values from 40 to 160, as said below
Outputs:
- output: float32 [256, 32768], P('rep', ('row', 'col'))
- input_grad: float32 [256, 32768], P('rep', ('col', 'row'))
- weight_grad: float32 [256, 256], P('rep')
Inputs may be any that keep to these rules, and one draw needn't show every extreme that they name: `tile_count`: a block's slots at or after its count are not part of the adjacency; some block uses all 160 slots. `tile_row`: slots may repeat a tile position; their tiles add. `tile_kind`: an index into the 160 stored tiles of the same block.
All inputs are finite; a program needn't handle non-finite values.
Results may differ from a plain program's by a relative error of at most 0.0001.
Values sent between devices are 32-bit elements; how exact they have to be, the bound alone decides.
No kernel may reach another device: no remote copies, remote signals or barrier semaphores. Data moves between devices by JAX's collectives and lax.ppermute only.
A program may use at most 128 MiB of HBM per device.

v0:
```python
import jax
import jax.numpy as jnp
from jax import lax
from jax.sharding import PartitionSpec as P


def tile_terms(source, values, from_tile, to_tile, tile_kinds, live_weight, dest_tiles, transposed):
    feat_width = source.shape[0]
    tile_edge = values.shape[1]
    tiled = source.reshape(feat_width, source.shape[1] // tile_edge, tile_edge)
    picked = jnp.take(tiled, from_tile, axis=1)
    chosen = jnp.take(values, tile_kinds, axis=0)
    if transposed:
        products = jnp.einsum("fga,gab->fgb", picked, chosen, precision=lax.Precision.HIGHEST)
    else:
        products = jnp.einsum("fgb,gab->fga", picked, chosen, precision=lax.Precision.HIGHEST)
    onehot = (to_tile[:, None] == jnp.arange(dest_tiles, dtype=jnp.int32)[None, :]).astype(
        jnp.float32
    )
    onehot = onehot * live_weight[:, None]
    spread = jnp.einsum("fgt,gd->fdt", products, onehot, precision=lax.Precision.HIGHEST)
    return spread.reshape(feat_width, dest_tiles * tile_edge)


def aggregate(source, values, from_tile, to_tile, tile_kinds, live_count, dest_tiles, transposed):
    slot_total = tile_kinds.shape[0]
    live_weight = (jnp.arange(slot_total, dtype=jnp.int32) < live_count).astype(jnp.float32)
    return tile_terms(
        source, values, from_tile, to_tile, tile_kinds, live_weight, dest_tiles, transposed
    )


def local(features, weight, cotangent, tile_values, tile_row, tile_col, tile_kind, tile_count):
    n_rowdev = lax.axis_size("row")
    n_coldev = lax.axis_size("col")
    n_repdev = lax.axis_size("rep")
    quarter = weight.shape[0] // n_repdev
    rep_index = lax.axis_index("rep")
    own_rows = lax.dynamic_slice_in_dim(weight, rep_index * quarter, quarter, 0)
    own_cols = lax.dynamic_slice_in_dim(weight, rep_index * quarter, quarter, 1)
    stretch_len = features.shape[1]
    tile_edge = tile_values.shape[1]
    live_count = tile_count[0]
    row_tiles = n_coldev * stretch_len // tile_edge
    col_tiles = n_rowdev * stretch_len // tile_edge
    mixed = lax.psum_scatter(
        lax.dot_general(
            own_rows,
            features,
            (((0,), (0,)), ((), ())),
            precision=lax.Precision.HIGHEST,
            preferred_element_type=jnp.float32,
        ),
        "rep",
        scatter_dimension=0,
        tiled=True,
    )
    column_block = lax.all_gather(mixed, "row", axis=1, tiled=True)
    partial_value = aggregate(
        column_block, tile_values, tile_col, tile_row, tile_kind, live_count, row_tiles, False
    )
    summed = lax.psum_scatter(partial_value, "col", scatter_dimension=1, tiled=True)
    output, pullback = jax.vjp(lambda v: jax.nn.gelu(v, approximate=True), summed)
    (grad_pre,) = pullback(cotangent)
    row_block = lax.all_gather(grad_pre, "col", axis=1, tiled=True)
    partial_back = aggregate(
        row_block, tile_values, tile_row, tile_col, tile_kind, live_count, col_tiles, True
    )
    grad_mixed = lax.psum_scatter(partial_back, "row", scatter_dimension=1, tiled=True)
    input_grad = lax.psum_scatter(
        jnp.dot(
            own_cols,
            grad_mixed,
            preferred_element_type=jnp.float32,
            precision=lax.Precision.HIGHEST,
        ),
        "rep",
        scatter_dimension=0,
        tiled=True,
    )
    weight_part = lax.dot_general(
        features,
        lax.all_gather(grad_mixed, "rep", axis=0, tiled=True),
        (((1,), (1,)), ((), ())),
        precision=lax.Precision.HIGHEST,
        preferred_element_type=jnp.float32,
    )
    node_total = stretch_len * n_rowdev * n_coldev
    weight_grad = lax.psum(weight_part * float(node_total) ** (-0.5), ("row", "col"))
    return (output, input_grad, weight_grad)


def solution(mesh):
    return jax.shard_map(
        local,
        mesh=mesh,
        in_specs=(
            P("rep", ("col", "row")),
            P(),
            P("rep", ("row", "col")),
            P(("row", "col"), None, None),
            P(("row", "col")),
            P(("row", "col")),
            P(("row", "col")),
            P(("row", "col")),
        ),
        out_specs=(P("rep", ("row", "col")), P("rep", ("col", "row")), P("rep", None)),
        check_vma=False,
    )
```

profile of v0, /device:TPU:2, one launch (start us, length us, event | category | flops | bytes accessed | tf_op | source)
XLA Modules:
  0.0 1082.4 jit_solution(2901445615518222513)
XLA Ops:
  8.1 2.3 fusion.39
  10.5 30.2 %reduce-scatter.5.cloned.1.call-done = f32[64,512]{1,0:T(8,128)} async-done(((f32[256,512]{1,0:T(8,128)}), f32[64,512]{1,0:T(8,128)}) %reduce-scatter.5.cloned.1.call-update) | async-done | bytes 131088 | tf_op jit(solution)/shard_map/reduce_scatter | solution.py:46
  42.1 14.2 %gather_fusion = f32[160,128,128]{2,1,0:T(8,128)} fusion(f32[160,128,128]{2,1,0:T(8,128)} %param.15, s32[1024]{0:T(1024)S(1)} %pad_clamp_fusion.2), kind=kCustom, calls=%fused_computation.clone | custom fusion | bytes 20972160 | tf_op jit(solution)/shard_map/jit(_take)/gather | solution.py:12
  56.3 10.5 all-gather.3.cloned.1.call-done
  66.8 1.3 copy_bitcast_fusion.3
  68.2 3.3 gather_fusion.1
  71.5 24.3 %fusion.20 = f32[64,160,128]{2,0,1:T(8,128)S(1)} fusion(f32[160,64,128]{2,1,0:T(8,128)} %gather_fusion.1, pred[160]{0:T(512)(128)(4,1)S(1)} %get-tuple-element.7, f32[160,128,128]{2,1,0:T(8,128)} %gather_fusion, pred[160]{0:T(512)(128)(4,1)S(1)} %get-tuple-element.8), kind=kOutput, calls=%fused_computation.23 | convolution fusion | flops 2017198080 | bytes 20971840 | tf_op jit(solution)/shard_map/fgb,gab->fga/dot_general | solution.py:16
  95.8 5.6 fusion.8
  101.5 1.6 copy.29
  103.1 87.2 %reduce-scatter.7.cloned.1.call-done = f32[64,512]{1,0:T(8,128)} async-done(((f32[64,4096]{1,0:T(8,128)}), f32[64,512]{1,0:T(8,128)}) %reduce-scatter.7.cloned.1.call-update) | async-done | bytes 131088 | tf_op jit(solution)/shard_map/reduce_scatter | solution.py:62
  190.4 1.7 fusion.36
  192.2 59.1 %all-gather.5.cloned.1.call-done = f32[64,4096]{1,0:T(8,128)} async-done(((f32[64,512]{1,0:T(8,128)}), f32[64,4096]{1,0:T(8,128)}) %all-gather.5.cloned.1.call-update) | async-done | bytes 1048592 | tf_op jit(solution)/shard_map/all_gather | solution.py:65
  251.3 1.3 copy_bitcast_fusion.2
  252.7 3.3 gather_fusion.2
  255.9 13.9 %fusion.25 = f32[64,160,128]{2,0,1:T(8,128)S(1)} fusion(f32[160,64,128]{2,1,0:T(8,128)} %gather_fusion.2, pred[160]{0:T(512)(128)(4,1)S(1)} %compare_and_fusion, f32[160,128,128]{2,1,0:T(8,128)} %gather_fusion, pred[160]{0:T(512)(128)(4,1)S(1)} %get-tuple-element.8), kind=kOutput, calls=%fused_computation.24 | convolution fusion | flops 2017198080 | bytes 20971840 | tf_op jit(solution)/shard_map/fga,gab->fgb/dot_general | solution.py:14
  269.8 5.6 fusion.6
  275.5 1.6 copy.28
  277.1 30.8 %reduce-scatter.9.cloned.1.call-done = f32[64,512]{1,0:T(8,128)} async-done(((f32[64,4096]{1,0:T(8,128)}), f32[64,512]{1,0:T(8,128)}) %reduce-scatter.9.cloned.1.call-update) | async-done | bytes 131088 | tf_op jit(solution)/shard_map/reduce_scatter | solution.py:69
  307.9 16.4 %all_gather.11 = f32[256,512]{1,0:T(8,128)S(1)} all-gather(f32[64,512]{1,0:T(8,128)} %reduce-scatter.9.cloned.1.call-done), channel_id=1, replica_groups=mesh['row'=8,'col'=8,'rep'=4] {'rep'}, dimensions={0}, use_global_device_ids=true | all-gather | bytes 655360 | tf_op jit(solution)/shard_map/all_gather | solution.py:83
  324.4 1.2 fusion.30
  325.7 2.3 fusion.37
  328.0 722.2 %all-reduce.2.cloned.1.call-done = f32[64,256]{1,0:T(8,128)} async-done(((f32[64,256]{1,0:T(8,128)}), f32[64,256]{1,0:T(8,128)}) %all-reduce.2.cloned.1.call-update) | async-done | bytes 65552 | tf_op jit(solution)/shard_map/psum | solution.py:89
  1050.2 23.9 %reduce-scatter.11.cloned.1.call-done = f32[64,512]{1,0:T(8,128)} async-done(((f32[256,512]{1,0:T(8,128)}), f32[64,512]{1,0:T(8,128)}) %reduce-scatter.11.cloned.1.call-update) | async-done | bytes 131088 | tf_op jit(solution)/shard_map/reduce_scatter | solution.py:70
  1074.1 1.5 copy.32
  (35 shorter events, 2.1 us)
Async XLA Ops:
  7.2 1.0 copy-start
  7.2 33.5 %reduce-scatter.5.cloned.1.call-start = ((), (), s32[]{:S(2)}) async-start(), calls=%async_computation.4 | async-start | bytes 655360 | tf_op jit(solution)/shard_map/reduce_scatter | solution.py:46
  10.5 56.4 %all-gather.3.cloned.1.call-start = ((), (), s32[]{:S(2)}) async-start(), calls=%async_computation.5 | async-start | bytes 1179648 | tf_op jit(solution)/shard_map/all_gather | solution.py:58
  40.7 149.7 %reduce-scatter.7.cloned.1.call-start = ((), (), s32[]{:S(2)}) async-start(), calls=%async_computation.6 | async-start | bytes 1179648 | tf_op jit(solution)/shard_map/reduce_scatter | solution.py:62
  42.1 14.2 %copy-start.3 = (s32[160]{0:T(256)S(1)}, s32[160]{0:T(256)}, u32[]{:S(2)}) copy-start(s32[160]{0:T(256)} %param.17) | copy-start | bytes 1924
  42.1 14.2 %copy-start.5 = (s32[160]{0:T(256)S(1)}, s32[160]{0:T(256)}, u32[]{:S(2)}) copy-start(s32[160]{0:T(256)} %param.18) | copy-start | bytes 1924
  71.5 24.3 %copy-start.4 = (s32[160]{0:T(256)S(1)}, s32[160]{0:T(256)}, u32[]{:S(2)}) copy-start(s32[160]{0:T(256)} %param.16) | copy-start | bytes 1924
  95.8 94.6 %copy-start.2 = (f32[64,512]{1,0:T(8,128)S(1)}, f32[64,512]{1,0:T(8,128)}, u32[]{:S(2)}) copy-start(f32[64,512]{1,0:T(8,128)} %param.14) | copy-start | bytes 393220
  103.1 148.2 %all-gather.5.cloned.1.call-start = ((), (), s32[]{:S(2)}) async-start(), calls=%async_computation.7 | async-start | bytes 1179648 | tf_op jit(solution)/shard_map/all_gather | solution.py:65
  192.1 115.8 %reduce-scatter.9.cloned.1.call-start = ((), (), s32[]{:S(2)}) async-start(), calls=%async_computation.8 | async-start | bytes 1179648 | tf_op jit(solution)/shard_map/reduce_scatter | solution.py:69
  269.8 54.5 %copy-start.1 = (f32[64,512]{1,0:T(8,128)S(1)}, f32[64,512]{1,0:T(8,128)}, u32[]{:S(2)}) copy-start(f32[64,512]{1,0:T(8,128)} %param.12) | copy-start | bytes 393220
  277.1 773.1 %all-reduce.2.cloned.1.call-start = ((), (), s32[]{:S(2)}) async-start(), calls=%async_computation.10 | async-start | bytes 131072 | tf_op jit(solution)/shard_map/psum | solution.py:89
  325.6 748.5 %reduce-scatter.11.cloned.1.call-start = ((), (), s32[]{:S(2)}) async-start(), calls=%async_computation.9 | async-start | bytes 655360 | tf_op jit(solution)/shard_map/reduce_scatter | solution.py:70
Sparse Core Ops, SparseCore 0:
  10.6 30.0 reduce-scatter.4
  42.5 24.2 all-gather.2
  103.2 87.1 reduce-scatter.6
  193.4 57.8 all-gather.4
  277.2 30.6 reduce-scatter.8
  325.7 724.4 all-reduce.1
  1053.3 20.7 reduce-scatter.10
where the time goes:
time: 1080 us
  waiting for transfers between devices  964 us (89%)
  matrix products  55.3 us (5%)
  local copies, waits for them, and re-layouts  29 us (3%)
  blocking collectives  16.4 us (2%)
  between operations  14.9 us (1%)
    psum x1, waiting for transfers between devices, local(): lax.psum(weight_part * float(node_total) ** (-0.5), ('row', 'col'))  722 us
    reduce_scatter x1, waiting for transfers between devices, local(): lax.psum_scatter(partial_value, 'col', scatter_dimension=1, tiled=True)  87.2 us
    all_gather x1, waiting for transfers between devices, local(): row_block = lax.all_gather(grad_pre, 'col', axis=1, tiled=True)  59.1 us
    reduce_scatter x1, waiting for transfers between devices, local(): lax.psum_scatter(partial_back, 'row', scatter_dimension=1, tiled=True)  30.8 us
    reduce_scatter x1, waiting for transfers between devices, local(): lax.psum_scatter(lax.dot_general(own_rows, features, (((0,), (0,)), ((),...  30.2 us
    dot_general x1, matrix products, tile_terms(): jnp.einsum('fgb,gab->fga', picked, chosen, precision=lax.Precision.HIGHEST)  24.3 us
    reduce_scatter x1, waiting for transfers between devices, local(): lax.psum_scatter(jnp.dot(own_cols, grad_mixed, preferred_element_type=jnp...  23.9 us
  transfers between devices with their start and end apart: 7, of which 7 were waited for; matrix products, arithmetic and copies ran while one was open for 2% of the time, Pallas kernels for 0%

commit v1 on v0

--- a/solution.py
+++ b/solution.py
@@ -2,6 +2,7 @@
 import jax.numpy as jnp
 from jax import lax
 from jax.sharding import PartitionSpec as P
+from jax.lax import all_gather
 
 
 def tile_terms(source, values, from_tile, to_tile, tile_kinds, live_weight, dest_tiles, transposed):
@@ -86,7 +87,8 @@
         preferred_element_type=jnp.float32,
     )
     node_total = stretch_len * n_rowdev * n_coldev
-    weight_grad = lax.psum(weight_part * float(node_total) ** (-0.5), ("row", "col"))
+    wait_strings_in = lambda x_part: all_gather(x_part, axis_name=("row", "col")).sum(axis=0)
+    weight_grad = wait_strings_in(weight_part * float(node_total) ** (-0.5))
     return (output, input_grad, weight_grad)
 
 

time: 1080 us -> 447 us (0.41)
  waiting for transfers between devices: 964 us -> 327 us
    psum x1 -> x0, waiting for transfers between devices: 722 us -> none  [local(): lax.psum(weight_part * float(node_total) ** (-0.5), ('row', 'col'))]
    all_gather x0 -> x1, waiting for transfers between devices: none -> 86.8 us  [local(): all_gather(x_part, axis_name=('row', 'col')).sum(axis=0)]
  transfers between devices with their start and end apart: 7 -> 7, of which waited for: 7 -> 7; matrix products, arithmetic and copies ran while one was open for 2% -> 5% of each run, Pallas kernels for 0% -> 0%
where the time goes in v1:
time: 447 us
  waiting for transfers between devices  327 us (73%)
  matrix products  55.4 us (12%)
  local copies, waits for them, and re-layouts  27.5 us (6%)
  blocking collectives  16.4 us (4%)
  between operations  14.9 us (3%)
  other arithmetic  5.49 us (1%)
    reduce_scatter x1, waiting for transfers between devices, local(): lax.psum_scatter(partial_value, 'col', scatter_dimension=1, tiled=True)  87.2 us
    all_gather x1, waiting for transfers between devices, local(): all_gather(x_part, axis_name=('row', 'col')).sum(axis=0)  86.8 us
    all_gather x1, waiting for transfers between devices, local(): row_block = lax.all_gather(grad_pre, 'col', axis=1, tiled=True)  59.1 us
    reduce_scatter x1, waiting for transfers between devices, local(): lax.psum_scatter(partial_back, 'row', scatter_dimension=1, tiled=True)  30.8 us
    reduce_scatter x1, waiting for transfers between devices, local(): lax.psum_scatter(lax.dot_general(own_rows, features, (((0,), (0,)), ((),...  30.2 us
    dot_general x1, matrix products, tile_terms(): jnp.einsum('fgb,gab->fga', picked, chosen, precision=lax.Precision.HIGHEST)  24.3 us
    reduce_scatter x1, waiting for transfers between devices, local(): lax.psum_scatter(jnp.dot(own_cols, grad_mixed, preferred_element_type=jnp...  22.3 us
    all_gather x1, blocking collectives, local(): lax.all_gather(grad_mixed, 'rep', axis=0, tiled=True)  16.4 us
  transfers between devices with their start and end apart: 7, of which 7 were waited for; matrix products, arithmetic and copies ran while one was open for 5% of the time, Pallas kernels for 0%

profile of v1, /device:TPU:2, one launch (start us, length us, event | category | flops | bytes accessed | tf_op | source)
XLA Modules:
  0.0 447.0 jit_solution(1629889419929185207)
XLA Ops:
  8.1 2.3 fusion.39
  10.5 30.2 %reduce-scatter.5.cloned.1.call-done = f32[64,512]{1,0:T(8,128)} async-done(((f32[256,512]{1,0:T(8,128)}), f32[64,512]{1,0:T(8,128)}) %reduce-scatter.5.cloned.1.call-update) | async-done | bytes 131088 | tf_op jit(solution)/shard_map/reduce_scatter | solution.py:47
  42.1 14.2 %gather_fusion = f32[160,128,128]{2,1,0:T(8,128)} fusion(f32[160,128,128]{2,1,0:T(8,128)} %param.15, s32[1024]{0:T(1024)S(1)} %pad_clamp_fusion.2), kind=kCustom, calls=%fused_computation.clone | custom fusion | bytes 20972160 | tf_op jit(solution)/shard_map/jit(_take)/gather | solution.py:13
  56.3 10.5 %all-gather.5.cloned.1.call-done = f32[64,4096]{1,0:T(8,128)} async-done(((f32[64,512]{1,0:T(8,128)}), f32[64,4096]{1,0:T(8,128)}) %all-gather.5.cloned.1.call-update) | async-done | bytes 1048592 | tf_op jit(solution)/shard_map/all_gather | solution.py:59
  66.8 1.3 copy_bitcast_fusion.3
  68.2 3.3 gather_fusion.1
  71.5 24.3 %fusion.20 = f32[64,160,128]{2,0,1:T(8,128)S(1)} fusion(f32[160,64,128]{2,1,0:T(8,128)} %gather_fusion.1, pred[160]{0:T(512)(128)(4,1)S(1)} %get-tuple-element.7, f32[160,128,128]{2,1,0:T(8,128)} %gather_fusion, pred[160]{0:T(512)(128)(4,1)S(1)} %get-tuple-element.8), kind=kOutput, calls=%fused_computation.23 | convolution fusion | flops 2017198080 | bytes 20971840 | tf_op jit(solution)/shard_map/fgb,gab->fga/dot_general | solution.py:17
  95.8 5.6 %fusion.8 = f32[32,64,128]{2,0,1:T(8,128)S(1)} fusion(f32[64,160,128]{2,0,1:T(8,128)S(1)} %fusion.20, f32[160]{0:T(256)S(1)} %compare_convert_fusion, s32[160]{0:T(256)S(1)} %copy-done.4), kind=kOutput, calls=%fused_computation.11 | convolution fusion | flops 503326720 | bytes 6292736 | tf_op jit(solution)/shard_map/fgt,gd->fdt/dot_general | solution.py:22
  101.5 1.6 copy.29
  103.1 87.2 %reduce-scatter.7.cloned.1.call-done = f32[64,512]{1,0:T(8,128)} async-done(((f32[64,4096]{1,0:T(8,128)}), f32[64,512]{1,0:T(8,128)}) %reduce-scatter.7.cloned.1.call-update) | async-done | bytes 131088 | tf_op jit(solution)/shard_map/reduce_scatter | solution.py:63
  190.4 1.7 fusion.36
  192.2 59.1 %all-gather.7.cloned.1.call-done = f32[64,4096]{1,0:T(8,128)} async-done(((f32[64,512]{1,0:T(8,128)}), f32[64,4096]{1,0:T(8,128)}) %all-gather.7.cloned.1.call-update) | async-done | bytes 1048592 | tf_op jit(solution)/shard_map/all_gather | solution.py:66
  251.3 1.3 copy_bitcast_fusion.2
  252.7 3.3 gather_fusion.2
  255.9 13.9 %fusion.25 = f32[64,160,128]{2,0,1:T(8,128)S(1)} fusion(f32[160,64,128]{2,1,0:T(8,128)} %gather_fusion.2, pred[160]{0:T(512)(128)(4,1)S(1)} %compare_and_fusion, f32[160,128,128]{2,1,0:T(8,128)} %gather_fusion, pred[160]{0:T(512)(128)(4,1)S(1)} %get-tuple-element.8), kind=kOutput, calls=%fused_computation.24 | convolution fusion | flops 2017198080 | bytes 20971840 | tf_op jit(solution)/shard_map/fga,gab->fgb/dot_general | solution.py:15
  269.8 5.6 %fusion.6 = f32[32,64,128]{2,0,1:T(8,128)S(1)} fusion(f32[64,160,128]{2,0,1:T(8,128)S(1)} %fusion.25, s32[160]{0:T(256)S(1)} %copy-done.3, f32[160]{0:T(256)S(1)} %compare_convert_fusion), kind=kOutput, calls=%fused_computation.9 | convolution fusion | flops 503326720 | bytes 6292736 | tf_op jit(solution)/shard_map/fgt,gd->fdt/dot_general | solution.py:22
  275.5 1.6 copy.28
  277.1 30.8 %reduce-scatter.9.cloned.1.call-done = f32[64,512]{1,0:T(8,128)} async-done(((f32[64,4096]{1,0:T(8,128)}), f32[64,512]{1,0:T(8,128)}) %reduce-scatter.9.cloned.1.call-update) | async-done | bytes 131088 | tf_op jit(solution)/shard_map/reduce_scatter | solution.py:70
  307.9 16.4 %all_gather.17 = f32[256,512]{1,0:T(8,128)S(1)} all-gather(f32[64,512]{1,0:T(8,128)} %reduce-scatter.9.cloned.1.call-done), channel_id=1, replica_groups=mesh['row'=8,'col'=8,'rep'=4] {'rep'}, dimensions={0}, use_global_device_ids=true | all-gather | bytes 655360 | tf_op jit(solution)/shard_map/all_gather | solution.py:84
  324.4 1.2 fusion.30
  325.7 2.3 fusion.37
  328.0 86.8 %all-gather.9.cloned.1.call-done = f32[4096,256]{1,0:T(8,128)} async-done(((f32[64,256]{1,0:T(8,128)}), f32[4096,256]{1,0:T(8,128)}) %all-gather.9.cloned.1.call-update) | async-done | bytes 4194320 | tf_op jit(solution)/shard_map/all_gather | solution.py:90
  414.8 3.1 reduce_sum.9
  417.9 22.3 %reduce-scatter.11.cloned.1.call-done = f32[64,512]{1,0:T(8,128)} async-done(((f32[256,512]{1,0:T(8,128)}), f32[64,512]{1,0:T(8,128)}) %reduce-scatter.11.cloned.1.call-update) | async-done | bytes 131088 | tf_op jit(solution)/shard_map/reduce_scatter | solution.py:71
  (35 shorter events, 2.1 us)
Async XLA Ops:
  7.2 1.0 copy-start
  7.2 33.5 %reduce-scatter.5.cloned.1.call-start = ((), (), s32[]{:S(2)}) async-start(), calls=%async_computation.4 | async-start | bytes 655360 | tf_op jit(solution)/shard_map/reduce_scatter | solution.py:47
  10.5 56.4 %all-gather.5.cloned.1.call-start = ((), (), s32[]{:S(2)}) async-start(), calls=%async_computation.5 | async-start | bytes 1179648 | tf_op jit(solution)/shard_map/all_gather | solution.py:59
  40.7 149.7 %reduce-scatter.7.cloned.1.call-start = ((), (), s32[]{:S(2)}) async-start(), calls=%async_computation.6 | async-start | bytes 1179648 | tf_op jit(solution)/shard_map/reduce_scatter | solution.py:63
  42.1 14.2 %copy-start.3 = (s32[160]{0:T(256)S(1)}, s32[160]{0:T(256)}, u32[]{:S(2)}) copy-start(s32[160]{0:T(256)} %param.17) | copy-start | bytes 1924
  42.1 14.2 %copy-start.5 = (s32[160]{0:T(256)S(1)}, s32[160]{0:T(256)}, u32[]{:S(2)}) copy-start(s32[160]{0:T(256)} %param.18) | copy-start | bytes 1924
  71.5 24.3 %copy-start.4 = (s32[160]{0:T(256)S(1)}, s32[160]{0:T(256)}, u32[]{:S(2)}) copy-start(s32[160]{0:T(256)} %param.16) | copy-start | bytes 1924
  95.8 94.6 %copy-start.2 = (f32[64,512]{1,0:T(8,128)S(1)}, f32[64,512]{1,0:T(8,128)}, u32[]{:S(2)}) copy-start(f32[64,512]{1,0:T(8,128)} %param.14) | copy-start | bytes 393220
  103.1 148.2 %all-gather.7.cloned.1.call-start = ((), (), s32[]{:S(2)}) async-start(), calls=%async_computation.7 | async-start | bytes 1179648 | tf_op jit(solution)/shard_map/all_gather | solution.py:66
  192.1 115.8 %reduce-scatter.9.cloned.1.call-start = ((), (), s32[]{:S(2)}) async-start(), calls=%async_computation.8 | async-start | bytes 1179648 | tf_op jit(solution)/shard_map/reduce_scatter | solution.py:70
  269.8 54.5 %copy-start.1 = (f32[64,512]{1,0:T(8,128)S(1)}, f32[64,512]{1,0:T(8,128)}, u32[]{:S(2)}) copy-start(f32[64,512]{1,0:T(8,128)} %param.12) | copy-start | bytes 393220
  277.1 137.7 %all-gather.9.cloned.1.call-start = ((), (), s32[]{:S(2)}) async-start(), calls=%async_computation.10 | async-start | bytes 4259840 | tf_op jit(solution)/shard_map/all_gather | solution.py:90
  325.6 114.5 %reduce-scatter.11.cloned.1.call-start = ((), (), s32[]{:S(2)}) async-start(), calls=%async_computation.9 | async-start | bytes 655360 | tf_op jit(solution)/shard_map/reduce_scatter | solution.py:71
Sparse Core Ops, SparseCore 0:
  10.6 30.0 reduce-scatter.4
  42.5 24.2 all-gather.4
  103.2 87.1 reduce-scatter.6
  193.4 57.8 all-gather.6
  277.2 30.6 reduce-scatter.8
  325.7 89.0 all-gather.8
  417.9 22.1 reduce-scatter.10
